TPU v7x, 32 devices: a whole 2x2x4 slice. The times are simulated.
32 devices in a mesh: dp: 2 (over x), ctx: 8 (over z, y), tp: 2 (over core).
Axes of the slice: x: 2, y: 2, z: 4, core: 2. Of those that a mesh axis runs over, the one named last changes fastest.
Arguments:
- inputs: bfloat16 [2, 4096, 1024], P('dp', 'tp', 'ctx'), may hold values from -6 to 6
- gate: bfloat16 [2, 4096, 1024], P('dp', 'tp', 'ctx'), may hold values from -6 to 6
- grad_out: bfloat16 [2, 4096, 1024], P('dp', 'tp', 'ctx'), may hold values from -0.125 to 0.125
- filters: float32 [4096, 1024], P('tp', 'ctx'), may hold values from -6 to 6
Outputs:
- grad_inputs: bfloat16 [2, 4096, 1024], P('dp', 'tp', 'ctx')
- grad_gate: bfloat16 [2, 4096, 1024], P('dp', 'tp', 'ctx')
- grad_filters: float32 [4096, 1024], P('tp', 'ctx')
All inputs are finite; a program needn't handle non-finite values.
Results may differ from a plain program's by a relative error of at most 0.001.
Values may be sent and summed in bfloat16 or wider, within the bound.
A program may use at most 128 MiB of HBM per device.

v0:
```python
import math
from functools import partial

import jax
import jax.numpy as jnp
import numpy as np
from jax import lax
from jax.experimental import pallas as pl
from jax.experimental.pallas import tpu as pltpu
from jax.sharding import PartitionSpec as P

BF16 = jnp.bfloat16
F32 = jnp.float32


def tables(groups, width):
    outer = 2 * groups
    total = outer * width
    freqs = groups + 1
    k1 = np.arange(freqs)[:, None, None]
    b = np.arange(width)[None, :, None]
    k2 = np.arange(width)[None, None, :]
    angle = 2.0 * math.pi * ((b * (k1 + outer * k2)) % total) / total
    cosine, sine = np.cos(angle), -np.sin(angle)
    top = np.concatenate([cosine, sine], axis=2)
    bottom = np.concatenate([-sine, cosine], axis=2)
    matrix = np.concatenate([top, bottom], axis=1).astype(np.float32)
    high = matrix.astype(BF16)
    low = (matrix - high.astype(np.float32)).astype(BF16)
    phase = 2.0 * math.pi * ((np.arange(freqs)[:, None] * np.arange(groups)[None, :]) % outer) / outer
    weight = np.full((freqs, 1), 2.0)
    weight[0] = weight[-1] = 1.0
    weight = weight / total
    coef = np.stack([np.cos(phase), -np.sin(phase), weight * np.cos(phase), -weight * np.sin(phase)], axis=1)
    return high, low, coef.reshape(freqs * 4, groups).astype(np.float32)


def split(value):
    high = value.astype(BF16)
    return high, (value - high.astype(F32)).astype(BF16)


def transform_kernel(coef, x_ref, dy_ref, gate_ref, f_ref, mh_ref, ml_ref, gi_ref, gg_ref, gf_ref, sig, a_hi, a_lo, spec, acc):
    groups, owned, width = x_ref.shape
    step = pl.program_id(0)
    rows = min(32, owned)
    chunks = owned // rows

    @pl.when(step == 0)
    def _():
        def fill(r, _):
            at = pl.ds(pl.multiple_of(r * rows, rows), rows)
            for a in range(groups):
                sig[0, a, at, :] = x_ref[a, at, :].astype(F32)
                sig[1, a, at, :] = dy_ref[a, at, :].astype(F32) * gate_ref[a, at, :].astype(F32)
                sig[2, a, at, :] = f_ref[a, at, :]
                for s in range(3):
                    acc[s, a, at, :] = jnp.zeros((rows, width), F32)
            return 0

        lax.fori_loop(0, chunks, fill, 0)

    base = step * 4

    def forward(r, _):
        at = pl.ds(pl.multiple_of(r * rows, rows), rows)
        for s in range(3):
            real = imag = None
            for a in range(groups):
                value = sig[s, a, at, :]
                re, im = value * coef[base, a], value * coef[base + 1, a]
                real = re if real is None else real + re
                imag = im if imag is None else imag + im
            a_hi[s, at, :width], a_lo[s, at, :width] = split(real)
            a_hi[s, at, width:], a_lo[s, at, width:] = split(imag)
        return 0

    lax.fori_loop(0, chunks, forward, 0)

    def multiply(contract):
        dims = (((1,), (contract,)), ((), ()))
        dot = partial(lax.dot_general, dimension_numbers=dims, preferred_element_type=F32)
        for s in range(3):
            high, low = a_hi[s], a_lo[s]
            spec[s] = dot(high, mh_ref[0]) + dot(low, mh_ref[0]) + dot(high, ml_ref[0])

    multiply(0)

    def pointwise(r, _):
        at = pl.ds(pl.multiple_of(r * rows, rows), rows)
        xr, xi = spec[0, at, :width], spec[0, at, width:]
        pr, pi = spec[1, at, :width], spec[1, at, width:]
        fr, fi = spec[2, at, :width], spec[2, at, width:]
        terms = (
            (fr * xr - fi * xi, fr * xi + fi * xr),
            (fr * pr + fi * pi, fr * pi - fi * pr),
            (xr * pr + xi * pi, xr * pi - xi * pr),
        )
        for s, (real, imag) in enumerate(terms):
            a_hi[s, at, :width], a_lo[s, at, :width] = split(real)
            a_hi[s, at, width:], a_lo[s, at, width:] = split(imag)
        return 0

    lax.fori_loop(0, chunks, pointwise, 0)
    multiply(1)

    def inverse(r, _):
        at = pl.ds(pl.multiple_of(r * rows, rows), rows)
        for s in range(3):
            real, imag = spec[s, at, :width], spec[s, at, width:]
            for a in range(groups):
                acc[s, a, at, :] += real * coef[base + 2, a] + imag * coef[base + 3, a]
        return 0

    lax.fori_loop(0, chunks, inverse, 0)

    @pl.when(step == pl.num_programs(0) - 1)
    def _():
        def finish(r, _):
            at = pl.ds(pl.multiple_of(r * rows, rows), rows)
            for a in range(groups):
                gg_ref[a, at, :] = (dy_ref[a, at, :].astype(F32) * acc[0, a, at, :]).astype(BF16)
                gi_ref[a, at, :] = acc[1, a, at, :].astype(BF16)
                gf_ref[a, at, :] = acc[2, a, at, :]
            return 0

        lax.fori_loop(0, chunks, finish, 0)


def transform(x, dy, gate, filters, interpret=False):
    groups, owned, width = x.shape
    high, low, coef = tables(groups, width)
    freqs = groups + 1
    whole = pl.BlockSpec((groups, owned, width), lambda k: (0, 0, 0))
    table = pl.BlockSpec((1, 2 * width, 2 * width), lambda k: (k, 0, 0))
    shape = (groups, owned, width)
    return pl.pallas_call(
        transform_kernel,
        grid=(freqs,),
        in_specs=[pl.BlockSpec(memory_space=pltpu.SMEM), whole, whole, whole, whole, table, table],
        out_specs=[whole, whole, whole],
        out_shape=[
            jax.ShapeDtypeStruct(shape, BF16),
            jax.ShapeDtypeStruct(shape, BF16),
            jax.ShapeDtypeStruct(shape, F32),
        ],
        scratch_shapes=[
            pltpu.VMEM((3, groups, owned, width), F32),
            pltpu.VMEM((3, owned, 2 * width), BF16),
            pltpu.VMEM((3, owned, 2 * width), BF16),
            pltpu.VMEM((3, owned, 2 * width), F32),
            pltpu.VMEM((3, groups, owned, width), F32),
        ],
        compiler_params=pltpu.CompilerParams(vmem_limit_bytes=48 * 1024 * 1024),
        interpret=interpret,
    )(coef, x, dy, gate, filters, high, low)


def shards(inputs, gate, grad_out, filters):
    groups = lax.axis_size("ctx")
    channels, width = inputs.shape[1:]
    owned = channels // groups
    swap = partial(lax.all_to_all, axis_name="ctx", split_axis=0, concat_axis=0, tiled=True)

    def blocks(array):
        return array.reshape(groups, owned, width)

    x, dy, g, f = (swap(blocks(v)) for v in (inputs, grad_out, gate, filters))
    gi, gg, gf = transform(x, dy, g, f)
    gf = swap(lax.psum(gf, "dp"))
    return (
        swap(gi).reshape(1, channels, width),
        swap(gg).reshape(1, channels, width),
        gf.reshape(channels, width),
    )


def solution(mesh):
    placed = (P("dp", "tp", "ctx"), P("dp", "tp", "ctx"), P("dp", "tp", "ctx"), P("tp", "ctx"))
    return jax.shard_map(
        shards,
        mesh=mesh,
        in_specs=placed,
        out_specs=(P("dp", "tp", "ctx"), P("dp", "tp", "ctx"), P("tp", "ctx")),
        check_vma=False,
    )
```

profile of v0, /device:TPU:0, one launch (start us, length us, event | category | flops | bytes accessed | tf_op | source)
XLA Modules:
  0.0 208.6 jit_solution(782360683340301920)
XLA Ops:
  7.2 0.0 copy-start.3
  7.2 0.0 copy-start.4
  7.2 22.0 %all_to_all.35.x_ref = bf16[8,256,128]{2,1,0:T(8,128)(2,1)S(1)} all-to-all(bf16[8,256,128]{2,1,0:T(8,128)(2,1)} %bitcast.11), channel_id=1, replica_groups=mesh['dp'=2,'ctx'=8,'tp'=2] {'ctx'}, dimensions={0} | all-to-all | bytes 1048576 | tf_op jit(solution)/shard_map/all_to_all | solution.py:168
  29.1 0.0 copy-start.2
  29.1 0.0 copy-done.3
  29.1 17.6 %all_to_all.36.gate_ref = bf16[8,256,128]{2,1,0:T(8,128)(2,1)S(1)} all-to-all(bf16[8,256,128]{2,1,0:T(8,128)(2,1)S(1)} %bitcast.12), channel_id=1, replica_groups=mesh['dp'=2,'ctx'=8,'tp'=2] {'ctx'}, dimensions={0} | all-to-all | bytes 1048576 | tf_op jit(solution)/shard_map/all_to_all | solution.py:168
  46.8 0.0 copy-done.4
  46.8 17.4 %all_to_all.37.dy_ref = bf16[8,256,128]{2,1,0:T(8,128)(2,1)S(1)} all-to-all(bf16[8,256,128]{2,1,0:T(8,128)(2,1)S(1)} %bitcast.13), channel_id=1, replica_groups=mesh['dp'=2,'ctx'=8,'tp'=2] {'ctx'}, dimensions={0} | all-to-all | bytes 1048576 | tf_op jit(solution)/shard_map/all_to_all | solution.py:168
  64.2 0.0 copy-start
  64.2 0.0 copy-start.1
  64.2 0.0 copy-done.2
  64.2 28.9 %all_to_all.38.f_ref = f32[8,256,128]{2,1,0:T(8,128)S(1)} all-to-all(f32[8,256,128]{2,1,0:T(8,128)S(1)} %bitcast.10), channel_id=1, replica_groups=mesh['dp'=2,'ctx'=8,'tp'=2] {'ctx'}, dimensions={0} | all-to-all | bytes 2097152 | tf_op jit(solution)/shard_map/all_to_all | solution.py:168
  93.1 0.0 copy-done
  93.1 0.0 copy-done.1
  93.1 26.0 %shard_map.94 = (bf16[8,256,128]{2,1,0:T(8,128)(2,1)}, bf16[8,256,128]{2,1,0:T(8,128)(2,1)S(1)}, f32[8,256,128]{2,1,0:T(8,128)}) custom-call(f32[36,8]{1,0:T(8,128)S(1)} %copy-done.1, bf16[8,256,128]{2,1,0:T(8,128)(2,1)S(1)} %all_to_all.35.x_ref, bf16[8,256,128]{2,1,0:T(8,128)(2,1)S(1)} %all_to_all.37.dy_ref, bf16[8,256,128]{2,1,0:T(8,128)(2,1)S(1)} %all_to_all.36.gate_ref, ...), custom_call_target="tpu_custom_call" | custom-call | tf_op jit(solution)/shard_map/pallas_call | solution.py:137
  119.1 3.5 %all-to-all-start.4 = ((bf16[8,256,128]{2,1,0:T(8,128)(2,1)}), bf16[8,256,128]{2,1,0:T(8,128)(2,1)S(1)}, u32[]{:S(2)}, u32[]{:S(2)}) async-start(bf16[8,256,128]{2,1,0:T(8,128)(2,1)} %get-tuple-element.6), calls=%async_computation.4 | async-start | bytes 1048576 | tf_op jit(solution)/shard_map/all_to_all | solution.py:172
  122.7 0.0 all-reduce.2.cloned.1.call-start
  122.7 0.7 all-reduce.2.cloned.1.call-update
  123.4 13.3 %all-to-all-done.4 = bf16[8,256,128]{2,1,0:T(8,128)(2,1)S(1)} async-done(((bf16[8,256,128]{2,1,0:T(8,128)(2,1)}), bf16[8,256,128]{2,1,0:T(8,128)(2,1)S(1)}, u32[]{:S(2)}, u32[]{:S(2)}) %all-to-all-start.4) | async-done | bytes 524320 | tf_op jit(solution)/shard_map/all_to_all | solution.py:172
  136.7 17.7 %all_to_all.39 = bf16[8,256,128]{2,1,0:T(8,128)(2,1)S(1)} all-to-all(bf16[8,256,128]{2,1,0:T(8,128)(2,1)S(1)} %get-tuple-element.7), channel_id=1, replica_groups=mesh['dp'=2,'ctx'=8,'tp'=2] {'ctx'}, dimensions={0} | all-to-all | bytes 1048576 | tf_op jit(solution)/shard_map/all_to_all | solution.py:173
  154.4 13.5 %all-reduce.2.cloned.1.call-done = f32[8,256,128]{2,1,0:T(8,128)} async-done(((f32[8,256,128]{2,1,0:T(8,128)}), f32[8,256,128]{2,1,0:T(8,128)}) %all-reduce.2.cloned.1.call-update) | async-done | bytes 1048592 | tf_op jit(solution)/shard_map/psum | solution.py:170
  167.9 5.5 %all-to-all-start.6 = ((f32[8,256,128]{2,1,0:T(8,128)}), f32[8,256,128]{2,1,0:T(8,128)S(1)}, u32[]{:S(2)}, u32[]{:S(2)}) async-start(f32[8,256,128]{2,1,0:T(8,128)} %all-reduce.2.cloned.1.call-done), calls=%async_computation.6 | async-start | bytes 2097152 | tf_op jit(solution)/shard_map/all_to_all | solution.py:170
  173.4 25.8 %all-to-all-done.6 = f32[8,256,128]{2,1,0:T(8,128)S(1)} async-done(((f32[8,256,128]{2,1,0:T(8,128)}), f32[8,256,128]{2,1,0:T(8,128)S(1)}, u32[]{:S(2)}, u32[]{:S(2)}) %all-to-all-start.6) | async-done | bytes 1048608 | tf_op jit(solution)/shard_map/all_to_all | solution.py:170
  199.2 0.8 copy.14
  200.0 0.8 copy.15
  200.7 1.0 copy.16
Async XLA Ops:
  7.2 22.0 %copy-start.3 = (bf16[1,2048,128]{2,1,0:T(8,128)(2,1)S(1)}, bf16[1,2048,128]{2,1,0:T(8,128)(2,1)}, u32[]{:S(2)}) copy-start(bf16[1,2048,128]{2,1,0:T(8,128)(2,1)} %param.8) | copy-start | bytes 1572868
  7.2 39.6 %copy-start.4 = (bf16[1,2048,128]{2,1,0:T(8,128)(2,1)S(1)}, bf16[1,2048,128]{2,1,0:T(8,128)(2,1)}, u32[]{:S(2)}) copy-start(bf16[1,2048,128]{2,1,0:T(8,128)(2,1)} %param.9) | copy-start | bytes 1572868
  29.1 35.1 %copy-start.2 = (f32[2048,128]{1,0:T(8,128)S(1)}, f32[2048,128]{1,0:T(8,128)}, u32[]{:S(2)}) copy-start(f32[2048,128]{1,0:T(8,128)} %param.10) | copy-start | bytes 3145732
  64.2 28.9 %copy-start = (bf16[9,256,256]{2,1,0:T(8,128)(2,1)S(1)}, bf16[9,256,256]{2,1,0:T(8,128)(2,1)}, u32[]{:S(2)}) copy-start(bf16[9,256,256]{2,1,0:T(8,128)(2,1)} %constant.7.clone.mh_ref) | copy-start | bytes 3538948
  64.2 28.9 %copy-start.1 = (f32[36,8]{1,0:T(8,128)S(1)}, f32[36,8]{1,0:T(8,128)}, u32[]{:S(2)}) copy-start(f32[36,8]{1,0:T(8,128)} %constant.6.clone.coef) | copy-start | bytes 3460
  119.1 17.6 %all-to-all-start.4 = ((bf16[8,256,128]{2,1,0:T(8,128)(2,1)}), bf16[8,256,128]{2,1,0:T(8,128)(2,1)S(1)}, u32[]{:S(2)}, u32[]{:S(2)}) async-start(bf16[8,256,128]{2,1,0:T(8,128)(2,1)} %get-tuple-element.6), calls=%async_computation.4 | async-start | bytes 1048576 | tf_op jit(solution)/shard_map/all_to_all | solution.py:172
  122.7 45.2 %all-reduce.2.cloned.1.call-start = ((), (), s32[]{:S(2)}) async-start(), calls=%async_computation.7 | async-start | bytes 2097152 | tf_op jit(solution)/shard_map/psum | solution.py:170
  167.9 31.3 %all-to-all-start.6 = ((f32[8,256,128]{2,1,0:T(8,128)}), f32[8,256,128]{2,1,0:T(8,128)S(1)}, u32[]{:S(2)}, u32[]{:S(2)}) async-start(f32[8,256,128]{2,1,0:T(8,128)} %all-reduce.2.cloned.1.call-done), calls=%async_computation.6 | async-start | bytes 2097152 | tf_op jit(solution)/shard_map/all_to_all | solution.py:170
Sparse Core Ops, SparseCore 0:
  126.4 41.4 all-reduce.1
where the time goes:
time: 209 us
  blocking collectives  104 us (50%)
  waiting for transfers between devices  53.2 us (25%)
  Pallas kernels  26 us (12%)
  between operations  14.1 us (7%)
  starting transfers between devices  9.1 us (4%)
  local copies, waits for them, and re-layouts  2.57 us (1%)
    all_to_all x4, blocking collectives, shards(): x, dy, g, f = (swap(blocks(v)) for v in (inputs, grad_out, gate, filters))  85.9 us
    pallas_call x1, Pallas kernels, transform(): pl.pallas_call(transform_kernel, grid=(freqs,), in_specs=[pl.BlockSpec(me...  26 us
    all_to_all x1, waiting for transfers between devices, shards(): gf = swap(lax.psum(gf, 'dp'))  25.8 us
    all_to_all x1, blocking collectives, shards(): swap(gg).reshape(1, channels, width)  17.7 us
    psum x1, waiting for transfers between devices, shards(): gf = swap(lax.psum(gf, 'dp'))  13.5 us
    all_to_all x1, waiting for transfers between devices, shards(): swap(gi).reshape(1, channels, width)  13.3 us
    all_to_all x1, starting transfers between devices, shards(): gf = swap(lax.psum(gf, 'dp'))  5.52 us
  transfers between devices with their start and end apart: 3, of which 3 were waited for; matrix products, arithmetic and copies ran while one was open for 0% of the time, Pallas kernels for 0%

commit v1 on v0

--- a/solution.py
+++ b/solution.py
@@ -11,6 +11,7 @@
 
 BF16 = jnp.bfloat16
 F32 = jnp.float32
+MESH = pl.DeviceIdType.MESH
 
 
 def tables(groups, width):
@@ -156,21 +157,240 @@
     )(coef, x, dy, gate, filters, high, low)
 
 
+def greet(me, groups, twin):
+    barrier = pltpu.get_barrier_semaphore()
+
+    def hail(o, _):
+        pl.semaphore_signal(barrier, inc=1, device_id={"ctx": lax.rem(me + o, groups)}, device_id_type=MESH)
+        return 0
+
+    lax.fori_loop(1, groups, hail, 0)
+    pl.semaphore_signal(barrier, inc=1, device_id={"dp": twin}, device_id_type=MESH)
+    pl.semaphore_wait(barrier, groups)
+
+
+def gather_kernel(groups, *refs):
+    sources, targets = refs[:4], refs[4:8]
+    send, recv, pass_send, pass_recv, local = refs[8:]
+    owned = sources[0].shape[1]
+    half = owned // 2
+    me, dp = lax.axis_index("ctx"), lax.axis_index("dp")
+    twin = 1 - dp
+    mine = pl.ds(pl.multiple_of(dp * half, half), half)
+    theirs = pl.ds(pl.multiple_of(twin * half, half), half)
+
+    def push(s, peer, slot, sem):
+        source, target = sources[s].at[peer], targets[s].at[slot]
+        if s == 0:
+            source, target = sources[0].at[peer, mine], targets[0].at[slot, mine]
+        return pltpu.make_async_remote_copy(
+            src_ref=source,
+            dst_ref=target,
+            send_sem=send.at[s, peer],
+            recv_sem=recv.at[s, sem],
+            device_id={"ctx": peer},
+            device_id_type=MESH,
+        )
+
+    def hand(slot, rows):
+        return pltpu.make_async_remote_copy(
+            src_ref=targets[0].at[slot, rows],
+            dst_ref=targets[0].at[slot, rows],
+            send_sem=pass_send.at[slot],
+            recv_sem=pass_recv.at[slot],
+            device_id={"dp": twin},
+            device_id_type=MESH,
+        )
+
+    def keep(s):
+        return pltpu.make_async_copy(sources[s].at[me], targets[s].at[me], local.at[s])
+
+    greet(me, groups, twin)
+    for s in range(4):
+
+        def start(o, _):
+            push(s, lax.rem(me + o, groups), me, me).start()
+            return 0
+
+        lax.fori_loop(1, groups, start, 0)
+        keep(s).start()
+
+    def relay(o, _):
+        origin = lax.rem(me + groups - o, groups)
+        push(0, origin, origin, origin).wait_recv()
+        hand(origin, mine).start()
+        return 0
+
+    lax.fori_loop(1, groups, relay, 0)
+    for s in range(4):
+
+        def finish(o, _):
+            origin = lax.rem(me + groups - o, groups)
+            if s:
+                push(s, origin, origin, origin).wait_recv()
+            else:
+                hand(origin, mine).wait_send()
+                hand(origin, theirs).wait_recv()
+            push(s, origin, origin, origin).wait_send()
+            return 0
+
+        lax.fori_loop(1, groups, finish, 0)
+        keep(s).wait()
+
+
+def gather(filters, *signals):
+    groups = filters.shape[0]
+    arrays = (filters,) + signals
+    anywhere = pl.BlockSpec(memory_space=pl.ANY)
+    dma = pltpu.SemaphoreType.DMA
+    return pl.pallas_call(
+        partial(gather_kernel, groups),
+        in_specs=[anywhere] * 4,
+        out_specs=[anywhere] * 4,
+        out_shape=[jax.ShapeDtypeStruct(v.shape, v.dtype) for v in arrays],
+        scratch_shapes=[dma((4, groups)), dma((4, groups)), dma((groups,)), dma((groups,)), dma((4,))],
+        compiler_params=pltpu.CompilerParams(collective_id=0, has_side_effects=True),
+    )(*arrays)
+
+
+def scatter_kernel(groups, gf_ref, gi_ref, gg_ref, ogf_ref, ogi_ref, ogg_ref, inbox, total, *sems):
+    send, recv, twin_send, twin_recv, pass_send, pass_recv, local = sems
+    owned = gf_ref.shape[1]
+    half = owned // 2
+    me, dp = lax.axis_index("ctx"), lax.axis_index("dp")
+    twin = 1 - dp
+    mine = pl.ds(pl.multiple_of(dp * half, half), half)
+    theirs = pl.ds(pl.multiple_of(twin * half, half), half)
+    sources, targets = (total, gi_ref, gg_ref), (ogf_ref, ogi_ref, ogg_ref)
+
+    def push(s, peer, slot):
+        target = targets[s].at[slot]
+        if s == 0:
+            target = ogf_ref.at[slot, mine]
+        return pltpu.make_async_remote_copy(
+            src_ref=sources[s].at[peer],
+            dst_ref=target,
+            send_sem=send.at[s, peer],
+            recv_sem=recv.at[s, slot],
+            device_id={"ctx": peer},
+            device_id_type=MESH,
+        )
+
+    def trade(a):
+        return pltpu.make_async_remote_copy(
+            src_ref=gf_ref.at[a, theirs],
+            dst_ref=inbox.at[a],
+            send_sem=twin_send.at[a],
+            recv_sem=twin_recv.at[a],
+            device_id={"dp": twin},
+            device_id_type=MESH,
+        )
+
+    def hand(source, slot, rows):
+        return pltpu.make_async_remote_copy(
+            src_ref=source,
+            dst_ref=ogf_ref.at[slot, rows],
+            send_sem=pass_send.at[slot],
+            recv_sem=pass_recv.at[slot],
+            device_id={"dp": twin},
+            device_id_type=MESH,
+        )
+
+    def keep(s):
+        target = ogf_ref.at[me, mine] if s == 0 else targets[s].at[me]
+        return pltpu.make_async_copy(sources[s].at[me], target, local.at[s])
+
+    greet(me, groups, twin)
+
+    def open_trade(o, _):
+        trade(lax.rem(me + o, groups)).start()
+        return 0
+
+    lax.fori_loop(1, groups + 1, open_trade, 0)
+    for s in (1, 2):
+
+        def start(o, _):
+            push(s, lax.rem(me + o, groups), me).start()
+            return 0
+
+        lax.fori_loop(1, groups, start, 0)
+        keep(s).start()
+
+    def add(a):
+        trade(a).wait_recv()
+        total[a] = gf_ref[a, mine, :] + inbox[a]
+
+    def reduce(o, _):
+        peer = lax.rem(me + o, groups)
+        add(peer)
+        push(0, peer, me).start()
+        return 0
+
+    lax.fori_loop(1, groups, reduce, 0)
+    add(me)
+    keep(0).start()
+    hand(total.at[me], me, mine).start()
+
+    def relay(o, _):
+        origin = lax.rem(me + groups - o, groups)
+        push(0, origin, origin).wait_recv()
+        hand(ogf_ref.at[origin, mine], origin, mine).start()
+        return 0
+
+    lax.fori_loop(1, groups, relay, 0)
+
+    def settle(a, _):
+        trade(a).wait_send()
+        hand(total.at[me], a, mine).wait_send()
+        hand(total.at[me], a, theirs).wait_recv()
+        return 0
+
+    lax.fori_loop(0, groups, settle, 0)
+    for s in range(3):
+
+        def finish(o, _):
+            origin = lax.rem(me + groups - o, groups)
+            if s:
+                push(s, origin, origin).wait_recv()
+            push(s, origin, origin).wait_send()
+            return 0
+
+        lax.fori_loop(1, groups, finish, 0)
+        keep(s).wait()
+
+
+def scatter(gf, gi, gg):
+    groups, owned, width = gf.shape
+    arrays = (gf, gi, gg)
+    anywhere = pl.BlockSpec(memory_space=pl.ANY)
+    vmem = pl.BlockSpec(memory_space=pltpu.VMEM)
+    dma = pltpu.SemaphoreType.DMA
+    return pl.pallas_call(
+        partial(scatter_kernel, groups),
+        in_specs=[vmem, anywhere, anywhere],
+        out_specs=[anywhere] * 3,
+        out_shape=[jax.ShapeDtypeStruct(v.shape, v.dtype) for v in arrays],
+        scratch_shapes=[pltpu.VMEM((groups, owned // 2, width), F32)] * 2
+        + [dma((3, groups)), dma((3, groups))]
+        + [dma((groups,))] * 4
+        + [dma((3,))],
+        compiler_params=pltpu.CompilerParams(collective_id=1, has_side_effects=True),
+    )(*arrays)
+
+
 def shards(inputs, gate, grad_out, filters):
     groups = lax.axis_size("ctx")
     channels, width = inputs.shape[1:]
     owned = channels // groups
-    swap = partial(lax.all_to_all, axis_name="ctx", split_axis=0, concat_axis=0, tiled=True)
-
     def blocks(array):
         return array.reshape(groups, owned, width)
 
-    x, dy, g, f = (swap(blocks(v)) for v in (inputs, grad_out, gate, filters))
+    f, x, dy, g = gather(*(blocks(v) for v in (filters, inputs, grad_out, gate)))
     gi, gg, gf = transform(x, dy, g, f)
-    gf = swap(lax.psum(gf, "dp"))
+    gf, gi, gg = scatter(gf, gi, gg)
     return (
-        swap(gi).reshape(1, channels, width),
-        swap(gg).reshape(1, channels, width),
+        gi.reshape(1, channels, width),
+        gg.reshape(1, channels, width),
         gf.reshape(channels, width),
     )
 

time: 209 us -> 135 us (0.65)
  blocking collectives: 104 us -> 0 us
  Pallas kernels: 26 us -> 122 us
  waiting for transfers between devices: 53.2 us -> 0 us
  between operations: 14.1 us -> 0.72 us
  local copies, waits for them, and re-layouts: 2.57 us -> 11.7 us
  starting transfers between devices: 9.1 us -> 0 us
    all_to_all x5 -> x0, blocking collectives: 104 us -> none  [the longest x4 85.9 us: shards(): x, dy, g, f = (swap(blocks(v)) for v in (inputs, grad_out, gate, filters))]
    pallas_call x0 -> x2, Pallas kernels: none -> 97.2 us  [the longest x1 50 us: gather(): pl.pallas_call(partial(gather_kernel, groups), in_specs=[anywhere] * 4, o...]
    all_to_all x2 -> x0, waiting for transfers between devices: 39.1 us -> none  [the longest x1 25.8 us: shards(): gf = swap(lax.psum(gf, 'dp'))]
    psum x1 -> x0, waiting for transfers between devices: 13.5 us -> none  [shards(): gf = swap(lax.psum(gf, 'dp'))]
    unnamed x13 -> x23, local copies, waits for them, and re-layouts: 2.57 us -> 11.7 us
    all_to_all x2 -> x0, starting transfers between devices: 9.07 us -> none  [the longest x1 5.52 us: shards(): gf = swap(lax.psum(gf, 'dp'))]
  transfers between devices with their start and end apart: 3 -> 0, of which waited for: 3 -> 0; matrix products, arithmetic and copies ran while one was open for 0% -> 0% of each run, Pallas kernels for 0% -> 0%
where the time goes in v1:
time: 135 us; the launch traced here: 134 us
  Pallas kernels  122 us (90%)
  local copies, waits for them, and re-layouts  11.7 us (9%)
    pallas_call x1, Pallas kernels, gather(): pl.pallas_call(partial(gather_kernel, groups), in_specs=[anywhere] * 4, o...  50 us
    pallas_call x1, Pallas kernels, scatter(): pl.pallas_call(partial(scatter_kernel, groups), in_specs=[vmem, anywhere,...  47.1 us
    pallas_call x1, Pallas kernels, transform(): pl.pallas_call(transform_kernel, grid=(freqs,), in_specs=[pl.BlockSpec(me...  24.9 us
    unnamed x23, local copies, waits for them, and re-layouts  11.7 us

profile of v1, /device:TPU:0, one launch (start us, length us, event | category | flops | bytes accessed | tf_op | source)
XLA Modules:
  0.0 134.5 jit_solution(43631235371723249)
XLA Ops:
  0.6 0.0 copy-start
  0.6 0.0 copy-start.8
  0.7 50.0 %shard_map.94 = (f32[8,256,128]{2,1,0:T(8,128)}, bf16[8,256,128]{2,1,0:T(8,128)(2,1)}, bf16[8,256,128]{2,1,0:T(8,128)(2,1)}, bf16[8,256,128]{2,1,0:T(8,128)(2,1)}) custom-call(f32[8,256,128]{2,1,0:T(8,128)} %bitcast.7, bf16[8,256,128]{2,1,0:T(8,128)(2,1)} %bitcast.9, bf16[8,256,128]{2,1,0:T(8,128)(2,1)} %bitcast.10, bf16[8,256,128]{2,1,0:T(8,128)(2,1)} %bitcast.11), custom_call_target="tpu_custom_call" | custom-call | tf_op jit(solution)/shard_map/pallas_call | solution.py:246
  50.7 0.0 copy-done
  50.7 0.0 copy-done.8
  50.7 0.0 copy-start.2
  50.7 1.2 copy-done.2
  51.9 0.0 copy-start.5
  51.9 1.0 copy-done.5
  53.0 0.0 copy-start.6
  53.0 1.0 copy-done.6
  54.0 0.0 copy-start.7
  54.0 1.0 copy-done.7
  55.1 24.9 %shard_map.95 = (bf16[8,256,128]{2,1,0:T(8,128)(2,1)S(1)}, bf16[8,256,128]{2,1,0:T(8,128)(2,1)S(1)}, f32[8,256,128]{2,1,0:T(8,128)S(1)}) custom-call(f32[36,8]{1,0:T(8,128)S(1)} %copy-done.8, bf16[8,256,128]{2,1,0:T(8,128)(2,1)S(1)} %copy-done.5, bf16[8,256,128]{2,1,0:T(8,128)(2,1)S(1)} %copy-done.6, bf16[8,256,128]{2,1,0:T(8,128)(2,1)S(1)} %copy-done.7, ...), custom_call_target="tpu_custom_call" | custom-call | tf_op jit(solution)/shard_map/pallas_call | solution.py:138
  79.9 0.0 copy-start.1
  79.9 1.0 copy-done.1
  80.9 0.0 copy-start.3
  80.9 0.8 copy-done.3
  81.7 0.0 copy-start.4
  81.7 0.8 copy-done.4
  82.5 47.1 %shard_map.96 = (f32[8,256,128]{2,1,0:T(8,128)}, bf16[8,256,128]{2,1,0:T(8,128)(2,1)}, bf16[8,256,128]{2,1,0:T(8,128)(2,1)}) custom-call(f32[8,256,128]{2,1,0:T(8,128)} %copy-done.1, bf16[8,256,128]{2,1,0:T(8,128)(2,1)} %copy-done.3, bf16[8,256,128]{2,1,0:T(8,128)(2,1)} %copy-done.4), custom_call_target="tpu_custom_call" | custom-call | tf_op jit(solution)/shard_map/pallas_call | solution.py:368
  129.6 0.0 copy-start.9
  129.7 2.0 %copy.13 = bf16[1,2048,128]{2,1,0:T(8,128)(2,1)} copy(bf16[1,2048,128]{2,1,0:T(8,128)(2,1)} %bitcast.13) | data formatting | bytes 1048576
  131.6 1.9 %copy.14 = bf16[1,2048,128]{2,1,0:T(8,128)(2,1)} copy(bf16[1,2048,128]{2,1,0:T(8,128)(2,1)} %bitcast.12) | data formatting | bytes 1048576
  133.5 0.0 copy-done.9
  133.5 1.0 copy.15
Async XLA Ops:
  0.6 50.1 %copy-start = (bf16[9,256,256]{2,1,0:T(8,128)(2,1)S(1)}, bf16[9,256,256]{2,1,0:T(8,128)(2,1)}, u32[]{:S(2)}) copy-start(bf16[9,256,256]{2,1,0:T(8,128)(2,1)} %constant.7.clone.mh_ref) | copy-start | bytes 3538948
  0.6 50.1 %copy-start.8 = (f32[36,8]{1,0:T(8,128)S(1)}, f32[36,8]{1,0:T(8,128)}, u32[]{:S(2)}) copy-start(f32[36,8]{1,0:T(8,128)} %constant.6.clone.coef) | copy-start | bytes 3460
  50.7 1.2 copy-start.2
  51.9 1.0 copy-start.5
  53.0 1.0 copy-start.6
  54.0 1.0 copy-start.7
  79.9 1.0 copy-start.1
  80.9 0.8 copy-start.3
  81.7 0.8 copy-start.4
  129.6 3.8 %copy-start.9 = (f32[8,256,128]{2,1,0:T(8,128)S(1)}, f32[8,256,128]{2,1,0:T(8,128)}, u32[]{:S(2)}) copy-start(f32[8,256,128]{2,1,0:T(8,128)} %get-tuple-element.22) | copy-start | bytes 3145732

commit v2 on v0

v2 whole, which is shorter than its diff:
```python
import math
from functools import partial

import jax
import jax.numpy as jnp
import numpy as np
from jax import lax
from jax.experimental import pallas as pl
from jax.experimental.pallas import tpu as pltpu
from jax.sharding import PartitionSpec as P

BF16 = jnp.bfloat16
F32 = jnp.float32
PARTS = 2
MESH = pl.DeviceIdType.MESH


def tables(groups, width):
    outer = 2 * groups
    total = outer * width
    freqs = groups + 1
    k1 = np.arange(freqs)[:, None, None]
    b = np.arange(width)[None, :, None]
    k2 = np.arange(width)[None, None, :]
    angle = 2.0 * math.pi * ((b * (k1 + outer * k2)) % total) / total
    cosine, sine = np.cos(angle), -np.sin(angle)
    top = np.concatenate([cosine, sine], axis=2)
    bottom = np.concatenate([-sine, cosine], axis=2)
    matrix = np.concatenate([top, bottom], axis=1).astype(np.float32)
    high = matrix.astype(BF16)
    low = (matrix - high.astype(np.float32)).astype(BF16)
    phase = 2.0 * math.pi * ((np.arange(freqs)[:, None] * np.arange(groups)[None, :]) % outer) / outer
    weight = np.full((freqs, 1), 2.0)
    weight[0] = weight[-1] = 1.0
    weight = weight / total
    coef = np.stack([np.cos(phase), -np.sin(phase), weight * np.cos(phase), -weight * np.sin(phase)], axis=1)
    return high, low, coef.reshape(freqs * 4, groups).astype(np.float32)


def split(value):
    high = value.astype(BF16)
    return high, (value - high.astype(F32)).astype(BF16)


def greet(me, groups, twin):
    barrier = pltpu.get_barrier_semaphore()

    def hail(o, _):
        pl.semaphore_signal(barrier, inc=1, device_id={"ctx": lax.rem(me + o, groups)}, device_id_type=MESH)
        return 0

    lax.fori_loop(1, groups, hail, 0)
    pl.semaphore_signal(barrier, inc=1, device_id={"dp": twin}, device_id_type=MESH)
    pl.semaphore_wait(barrier, groups)


def fused_kernel(groups, parts, coef, mh_ref, ml_ref, f_ref, x_ref, dy_ref, gate_ref, ogf_ref, ogi_ref, ogg_ref, *scratch):
    (filt, recv_sig, sig, a_hi, a_lo, spec, acc, gf, gi, gg, inbox, total) = scratch[:12]
    (f_send, f_recv, f_pass_send, f_pass_recv, x_send, x_recv, keep_sem) = scratch[12:19]
    (o_send, o_recv, twin_send, twin_recv, pass_send, pass_recv, out_sem) = scratch[19:]
    owned, width = f_ref.shape[1:]
    chunk = owned // parts
    half, slim = owned // 2, chunk // 2
    rows = min(32, chunk)
    pieces = chunk // rows
    me, dp = lax.axis_index("ctx"), lax.axis_index("dp")
    twin = 1 - dp
    sources = (x_ref, dy_ref, gate_ref)

    def f_rows(which):
        return pl.ds(pl.multiple_of(which * half, half), half)

    def part(q):
        return pl.ds(q * chunk, chunk)

    def slim_rows(q, which):
        return pl.ds(pl.multiple_of(q * chunk + which * slim, slim), slim)

    def remote(source, target, send, recv, device):
        return pltpu.make_async_remote_copy(
            src_ref=source, dst_ref=target, send_sem=send, recv_sem=recv, device_id=device, device_id_type=MESH
        )

    def f_push(peer, slot):
        return remote(
            f_ref.at[peer, f_rows(dp)], filt.at[slot, f_rows(dp)], f_send.at[peer], f_recv.at[slot], {"ctx": peer}
        )

    def f_hand(slot, which):
        block = filt.at[slot, f_rows(which)]
        return remote(block, block, f_pass_send.at[slot], f_pass_recv.at[slot], {"dp": twin})

    def x_push(s, q, peer, slot):
        return remote(
            sources[s].at[peer, part(q)],
            recv_sig.at[s, slot, part(q)],
            x_send.at[s, q, peer],
            x_recv.at[s, q, slot],
            {"ctx": peer},
        )

    def keep(s):
        if s == 3:
            return pltpu.make_async_copy(f_ref.at[me], filt.at[me], keep_sem.at[3])
        return pltpu.make_async_copy(sources[s].at[me], recv_sig.at[s, me], keep_sem.at[s])

    def trade(q, a):
        return remote(
            gf.at[a, slim_rows(q, twin)], inbox.at[q, a], twin_send.at[q, a], twin_recv.at[q, a], {"dp": twin}
        )

    def out_push(s, q, peer, slot):
        if s == 0:
            source, target = total.at[q, peer], ogf_ref.at[slot, slim_rows(q, dp)]
        else:
            source, target = (gi, gg)[s - 1].at[peer, part(q)], (ogi_ref, ogg_ref)[s - 1].at[slot, part(q)]
        return remote(source, target, o_send.at[s, q, peer], o_recv.at[s, q, slot], {"ctx": peer})

    def out_keep(s, q):
        if s == 0:
            return pltpu.make_async_copy(total.at[q, me], ogf_ref.at[me, slim_rows(q, dp)], out_sem.at[0, q])
        source, target = (gi, gg)[s - 1].at[me, part(q)], (ogi_ref, ogg_ref)[s - 1].at[me, part(q)]
        return pltpu.make_async_copy(source, target, out_sem.at[s, q])

    def hand(source, q, slot, which):
        return remote(
            source, ogf_ref.at[slot, slim_rows(q, which)], pass_send.at[q, slot], pass_recv.at[q, slot], {"dp": twin}
        )

    def each(first, body, last=groups):
        def run(o, _):
            body(lax.rem(me + o, groups), lax.rem(me + groups - o, groups))
            return 0

        lax.fori_loop(first, last, run, 0)

    def compute(q):
        def by_rows(body):
            def run(r, _):
                body(pl.multiple_of(r * rows, rows))
                return 0

            lax.fori_loop(0, pieces, run, 0)

        def fill(at):
            near, far = pl.ds(at, rows), pl.ds(pl.multiple_of(at + q * chunk, rows), rows)
            for a in range(groups):
                sig[0, a, near, :] = recv_sig[0, a, far, :].astype(F32)
                sig[1, a, near, :] = recv_sig[1, a, far, :].astype(F32) * recv_sig[2, a, far, :].astype(F32)
                sig[2, a, near, :] = filt[a, far, :]
                for s in range(3):
                    acc[s, a, near, :] = jnp.zeros((rows, width), F32)

        by_rows(fill)

        def frequency(k, _):
            base = k * 4

            def put(s, at, real, imag):
                to = pl.ds(pl.multiple_of(at + s * chunk, rows), rows)
                a_hi[to, :width], a_lo[to, :width] = split(real)
                a_hi[to, width:], a_lo[to, width:] = split(imag)

            def take(s, at):
                to = pl.ds(pl.multiple_of(at + s * chunk, rows), rows)
                return spec[to, :width], spec[to, width:]

            def forward(at):
                for s in range(3):
                    real = imag = None
                    for a in range(groups):
                        value = sig[s, a, pl.ds(at, rows), :]
                        re, im = value * coef[base, a], value * coef[base + 1, a]
                        real = re if real is None else real + re
                        imag = im if imag is None else imag + im
                    put(s, at, real, imag)

            def multiply(contract):
                dims = (((1,), (contract,)), ((), ()))
                dot = partial(lax.dot_general, dimension_numbers=dims, preferred_element_type=F32)
                high, low = a_hi[...], a_lo[...]
                spec[...] = dot(high, mh_ref[k]) + dot(low, mh_ref[k]) + dot(high, ml_ref[k])

            def pointwise(at):
                (xr, xi), (pr, pi), (fr, fi) = take(0, at), take(1, at), take(2, at)
                put(0, at, fr * xr - fi * xi, fr * xi + fi * xr)
                put(1, at, fr * pr + fi * pi, fr * pi - fi * pr)
                put(2, at, xr * pr + xi * pi, xr * pi - xi * pr)

            def inverse(at):
                for s in range(3):
                    real, imag = take(s, at)
                    for a in range(groups):
                        acc[s, a, pl.ds(at, rows), :] += real * coef[base + 2, a] + imag * coef[base + 3, a]

            by_rows(forward)
            multiply(0)
            by_rows(pointwise)
            multiply(1)
            by_rows(inverse)
            return 0

        lax.fori_loop(0, groups + 1, frequency, 0)

        def finish(at):
            near, far = pl.ds(at, rows), pl.ds(pl.multiple_of(at + q * chunk, rows), rows)
            for a in range(groups):
                gg[a, far, :] = (recv_sig[1, a, far, :].astype(F32) * acc[0, a, near, :]).astype(BF16)
                gi[a, far, :] = acc[1, a, near, :].astype(BF16)
                gf[a, far, :] = acc[2, a, near, :]

        by_rows(finish)

    greet(me, groups, twin)
    each(1, lambda to, origin: f_push(to, me).start())
    for q in range(parts):
        for s in range(3):
            each(1, lambda to, origin, s=s, q=q: x_push(s, q, to, me).start())
    for s in range(4):
        keep(s).start()

    def f_relay(to, origin):
        f_push(origin, origin).wait_recv()
        f_hand(origin, dp).start()

    each(1, f_relay)

    def f_settle(to, origin):
        f_hand(origin, dp).wait_send()
        f_hand(origin, twin).wait_recv()
        f_push(origin, origin).wait_send()

    each(1, f_settle)
    for s in range(4):
        keep(s).wait()
    for q in range(parts):
        for s in range(3):
            each(1, lambda to, origin, s=s, q=q: x_push(s, q, origin, origin).wait_recv())
        compute(q)
        each(1, lambda to, origin, q=q: trade(q, to).start(), groups + 1)
        for s in (1, 2):
            each(1, lambda to, origin, s=s, q=q: out_push(s, q, to, me).start())
            out_keep(s, q).start()

    for q in range(parts):

        def add(a, q=q):
            trade(q, a).wait_recv()
            total[q, a] = gf[a, slim_rows(q, dp), :] + inbox[q, a]

        def reduce(to, origin, q=q, add=add):
            add(to)
            out_push(0, q, to, me).start()

        each(1, reduce)
        add(me)
        out_keep(0, q).start()
        hand(total.at[q, me], q, me, dp).start()
    for q in range(parts):

        def relay(to, origin, q=q):
            out_push(0, q, origin, origin).wait_recv()
            hand(ogf_ref.at[origin, slim_rows(q, dp)], q, origin, dp).start()

        each(1, relay)
    for q in range(parts):

        def settle(a, origin, q=q):
            trade(q, a).wait_send()
            hand(total.at[q, me], q, a, dp).wait_send()
            hand(total.at[q, me], q, a, twin).wait_recv()

        each(1, settle, groups + 1)
        for s in range(3):

            def done(to, origin, q=q, s=s):
                x_push(s, q, origin, origin).wait_send()
                if s:
                    out_push(s, q, origin, origin).wait_recv()
                out_push(s, q, origin, origin).wait_send()

            each(1, done)
            out_keep(s, q).wait()


def fused(f, x, dy, gate):
    groups, owned, width = f.shape
    parts = PARTS if owned % (16 * PARTS) == 0 else 1
    chunk = owned // parts
    high, low, coef = tables(groups, width)
    anywhere = pl.BlockSpec(memory_space=pl.ANY)
    vmem = pl.BlockSpec(memory_space=pltpu.VMEM)
    dma = pltpu.SemaphoreType.DMA
    shape = (groups, owned, width)
    slim = (parts, groups, chunk // 2, width)
    return pl.pallas_call(
        partial(fused_kernel, groups, parts),
        in_specs=[pl.BlockSpec(memory_space=pltpu.SMEM), vmem, vmem] + [anywhere] * 4,
        out_specs=[anywhere] * 3,
        out_shape=[
            jax.ShapeDtypeStruct(shape, F32),
            jax.ShapeDtypeStruct(shape, BF16),
            jax.ShapeDtypeStruct(shape, BF16),
        ],
        scratch_shapes=[
            pltpu.VMEM(shape, F32),
            pltpu.VMEM((3,) + shape, BF16),
            pltpu.VMEM((3, groups, chunk, width), F32),
            pltpu.VMEM((3 * chunk, 2 * width), BF16),
            pltpu.VMEM((3 * chunk, 2 * width), BF16),
            pltpu.VMEM((3 * chunk, 2 * width), F32),
            pltpu.VMEM((3, groups, chunk, width), F32),
            pltpu.VMEM(shape, F32),
            pltpu.VMEM(shape, BF16),
            pltpu.VMEM(shape, BF16),
            pltpu.VMEM(slim, F32),
            pltpu.VMEM(slim, F32),
        ]
        + [dma((groups,))] * 4
        + [dma((3, parts, groups))] * 2
        + [dma((4,))]
        + [dma((3, parts, groups))] * 2
        + [dma((parts, groups))] * 4
        + [dma((3, parts))],
        compiler_params=pltpu.CompilerParams(
            collective_id=0, has_side_effects=True, vmem_limit_bytes=52 * 1024 * 1024
        ),
    )(coef, high, low, f, x, dy, gate)


def shards(inputs, gate, grad_out, filters):
    groups = lax.axis_size("ctx")
    channels, width = inputs.shape[1:]
    owned = channels // groups

    def blocks(array):
        return array.reshape(groups, owned, width)

    gf, gi, gg = fused(*(blocks(v) for v in (filters, inputs, grad_out, gate)))
    return (
        gi.reshape(1, channels, width),
        gg.reshape(1, channels, width),
        gf.reshape(channels, width),
    )


def solution(mesh):
    placed = (P("dp", "tp", "ctx"), P("dp", "tp", "ctx"), P("dp", "tp", "ctx"), P("tp", "ctx"))
    return jax.shard_map(
        shards,
        mesh=mesh,
        in_specs=placed,
        out_specs=(P("dp", "tp", "ctx"), P("dp", "tp", "ctx"), P("tp", "ctx")),
        check_vma=False,
    )
```

time: 209 us -> 114 us (0.55)
  the two profiles are of different devices: /device:TPU:0 before, /device:TPU:16 now
where the time goes in v2:
time: 114 us; the launch traced here: 113 us
  Pallas kernels  108 us (95%)
  local copies, waits for them, and re-layouts  4.32 us (4%)
    pallas_call x1, Pallas kernels, fused(): pl.pallas_call(partial(fused_kernel, groups, parts), in_specs=[pl.BlockSp...  108 us
    unnamed x9, local copies, waits for them, and re-layouts  4.32 us

profile of v2, /device:TPU:16, one launch (start us, length us, event | category | flops | bytes accessed | tf_op | source)
XLA Modules:
  0.0 113.5 jit_solution(2990389858370406606)
XLA Ops:
  0.6 0.0 copy-start
  0.6 1.0 copy-done
  1.7 0.0 copy-start.1
  1.7 0.7 copy-done.1
  2.4 108.5 %shard_map.94 = (f32[8,256,128]{2,1,0:T(8,128)}, bf16[8,256,128]{2,1,0:T(8,128)(2,1)S(1)}, bf16[8,256,128]{2,1,0:T(8,128)(2,1)S(1)}) custom-call(f32[36,8]{1,0:T(8,128)S(1)} %copy-done.1, bf16[9,256,256]{2,1,0:T(8,128)(2,1)} %constant.7.clone.mh_ref, bf16[9,256,256]{2,1,0:T(8,128)(2,1)} %constant.8.clone.ml_ref, f32[8,256,128]{2,1,0:T(8,128)} %bitcast.11, ...), custom_call_target="tpu_custom_call" | custom-call | tf_op jit(solution)/shard_map/pallas_call | solution.py:296
  110.9 0.0 copy-start.2
  110.9 0.8 copy.13
  111.7 0.8 copy.14
  112.5 0.0 copy-done.2
  112.5 1.0 copy.15
Async XLA Ops:
  0.6 1.0 copy-start
  1.7 0.7 copy-start.1
  110.9 1.6 %copy-start.2 = (f32[8,256,128]{2,1,0:T(8,128)S(1)}, f32[8,256,128]{2,1,0:T(8,128)}, u32[]{:S(2)}) copy-start(f32[8,256,128]{2,1,0:T(8,128)} %get-tuple-element.8) | copy-start | bytes 3145732

commit v3 on v2

--- a/solution.py
+++ b/solution.py
@@ -54,10 +54,11 @@
     pl.semaphore_wait(barrier, groups)
 
 
-def fused_kernel(groups, parts, coef, mh_ref, ml_ref, f_ref, x_ref, dy_ref, gate_ref, ogf_ref, ogi_ref, ogg_ref, *scratch):
+def fused_kernel(groups, parts, coef, high_ref, low_ref, f_ref, x_ref, dy_ref, gate_ref, ogf_ref, ogi_ref, ogg_ref, *scratch):
     (filt, recv_sig, sig, a_hi, a_lo, spec, acc, gf, gi, gg, inbox, total) = scratch[:12]
     (f_send, f_recv, f_pass_send, f_pass_recv, x_send, x_recv, keep_sem) = scratch[12:19]
-    (o_send, o_recv, twin_send, twin_recv, pass_send, pass_recv, out_sem) = scratch[19:]
+    (o_send, o_recv, twin_send, twin_recv, pass_send, pass_recv, out_sem) = scratch[19:26]
+    mh_ref, ml_ref, table_sem = scratch[26:]
     owned, width = f_ref.shape[1:]
     chunk = owned // parts
     half, slim = owned // 2, chunk // 2
@@ -134,7 +135,13 @@
 
         lax.fori_loop(first, last, run, 0)
 
-    def compute(q):
+    def load_tables():
+        return (
+            pltpu.make_async_copy(high_ref, mh_ref, table_sem.at[0]),
+            pltpu.make_async_copy(low_ref, ml_ref, table_sem.at[1]),
+        )
+
+    def compute(q, midway):
         def by_rows(body):
             def run(r, _):
                 body(pl.multiple_of(r * rows, rows))
@@ -200,7 +207,10 @@
             by_rows(inverse)
             return 0
 
-        lax.fori_loop(0, groups + 1, frequency, 0)
+        middle = (groups + 1) // 2 + 1
+        lax.fori_loop(0, middle, frequency, 0)
+        midway()
+        lax.fori_loop(middle, groups + 1, frequency, 0)
 
         def finish(at):
             near, far = pl.ds(at, rows), pl.ds(pl.multiple_of(at + q * chunk, rows), rows)
@@ -211,13 +221,27 @@
 
         by_rows(finish)
 
+    def combine(q):
+        def add(a):
+            trade(q, a).wait_recv()
+            total[q, a] = gf[a, slim_rows(q, dp), :] + inbox[q, a]
+
+        def reduce(to, origin):
+            add(to)
+            out_push(0, q, to, me).start()
+
+        each(1, reduce)
+        add(me)
+        out_keep(0, q).start()
+        hand(total.at[q, me], q, me, dp).start()
+
     greet(me, groups, twin)
     each(1, lambda to, origin: f_push(to, me).start())
     for q in range(parts):
         for s in range(3):
             each(1, lambda to, origin, s=s, q=q: x_push(s, q, to, me).start())
-    for s in range(4):
-        keep(s).start()
+    for copy in (*load_tables(), *(keep(s) for s in range(4))):
+        copy.start()
 
     def f_relay(to, origin):
         f_push(origin, origin).wait_recv()
@@ -231,31 +255,18 @@
         f_push(origin, origin).wait_send()
 
     each(1, f_settle)
-    for s in range(4):
-        keep(s).wait()
+    for copy in (*load_tables(), *(keep(s) for s in range(4))):
+        copy.wait()
     for q in range(parts):
         for s in range(3):
             each(1, lambda to, origin, s=s, q=q: x_push(s, q, origin, origin).wait_recv())
-        compute(q)
+        compute(q, partial(combine, q - 1) if q else lambda: None)
         each(1, lambda to, origin, q=q: trade(q, to).start(), groups + 1)
         for s in (1, 2):
             each(1, lambda to, origin, s=s, q=q: out_push(s, q, to, me).start())
             out_keep(s, q).start()
 
-    for q in range(parts):
-
-        def add(a, q=q):
-            trade(q, a).wait_recv()
-            total[q, a] = gf[a, slim_rows(q, dp), :] + inbox[q, a]
-
-        def reduce(to, origin, q=q, add=add):
-            add(to)
-            out_push(0, q, to, me).start()
-
-        each(1, reduce)
-        add(me)
-        out_keep(0, q).start()
-        hand(total.at[q, me], q, me, dp).start()
+    combine(parts - 1)
     for q in range(parts):
 
         def relay(to, origin, q=q):
@@ -289,13 +300,12 @@
     chunk = owned // parts
     high, low, coef = tables(groups, width)
     anywhere = pl.BlockSpec(memory_space=pl.ANY)
-    vmem = pl.BlockSpec(memory_space=pltpu.VMEM)
     dma = pltpu.SemaphoreType.DMA
     shape = (groups, owned, width)
     slim = (parts, groups, chunk // 2, width)
     return pl.pallas_call(
         partial(fused_kernel, groups, parts),
-        in_specs=[pl.BlockSpec(memory_space=pltpu.SMEM), vmem, vmem] + [anywhere] * 4,
+        in_specs=[pl.BlockSpec(memory_space=pltpu.SMEM)] + [anywhere] * 6,
         out_specs=[anywhere] * 3,
         out_shape=[
             jax.ShapeDtypeStruct(shape, F32),
@@ -321,7 +331,9 @@
         + [dma((4,))]
         + [dma((3, parts, groups))] * 2
         + [dma((parts, groups))] * 4
-        + [dma((3, parts))],
+        + [dma((3, parts))]
+        + [pltpu.VMEM(high.shape, BF16)] * 2
+        + [dma((2,))],
         compiler_params=pltpu.CompilerParams(
             collective_id=0, has_side_effects=True, vmem_limit_bytes=52 * 1024 * 1024
         ),

time: 114 us -> 106 us (0.930)
  the two profiles are of different devices: /device:TPU:16 before, /device:TPU:0 now
where the time goes in v3:
time: 106 us
  Pallas kernels  101 us (95%)
  local copies, waits for them, and re-layouts  4.32 us (4%)
    pallas_call x1, Pallas kernels, fused(): pl.pallas_call(partial(fused_kernel, groups, parts), in_specs=[pl.BlockSp...  101 us
    unnamed x9, local copies, waits for them, and re-layouts  4.32 us

profile of v3, /device:TPU:0, one launch (start us, length us, event | category | flops | bytes accessed | tf_op | source)
XLA Modules:
  0.0 105.6 jit_solution(13900299704675513706)
XLA Ops:
  0.6 0.0 copy-start
  0.6 1.0 copy-done
  1.7 0.0 copy-start.1
  1.7 0.7 copy-done.1
  2.4 100.7 %shard_map.94 = (f32[8,256,128]{2,1,0:T(8,128)}, bf16[8,256,128]{2,1,0:T(8,128)(2,1)S(1)}, bf16[8,256,128]{2,1,0:T(8,128)(2,1)S(1)}) custom-call(f32[36,8]{1,0:T(8,128)S(1)} %copy-done.1, bf16[9,256,256]{2,1,0:T(8,128)(2,1)} %constant.7.clone.high_ref, bf16[9,256,256]{2,1,0:T(8,128)(2,1)} %constant.8.clone.low_ref, f32[8,256,128]{2,1,0:T(8,128)} %bitcast.11, ...), custom_call_target="tpu_custom_call" | custom-call | tf_op jit(solution)/shard_map/pallas_call | solution.py:306
  103.1 0.0 copy-start.2
  103.1 0.8 copy.13
  103.9 0.8 copy.14
  104.7 0.0 copy-done.2
  104.7 1.0 copy.15
Async XLA Ops:
  0.6 1.0 copy-start
  1.7 0.7 copy-start.1
  103.1 1.6 %copy-start.2 = (f32[8,256,128]{2,1,0:T(8,128)S(1)}, f32[8,256,128]{2,1,0:T(8,128)}, u32[]{:S(2)}) copy-start(f32[8,256,128]{2,1,0:T(8,128)} %get-tuple-element.8) | copy-start | bytes 3145732

commit v4 on v3

--- a/solution.py
+++ b/solution.py
@@ -11,7 +11,7 @@
 
 BF16 = jnp.bfloat16
 F32 = jnp.float32
-PARTS = 2
+PARTS = 4
 MESH = pl.DeviceIdType.MESH
 
 

time: 106 us -> 101 us (0.953)
  Pallas kernels: 101 us -> 95.8 us
    pallas_call x1, Pallas kernels: 101 us -> 95.8 us  [fused(): pl.pallas_call(partial(fused_kernel, groups, parts), in_specs=[pl.BlockSp...]
where the time goes in v4:
time: 101 us
  Pallas kernels  95.8 us (95%)
  local copies, waits for them, and re-layouts  4.32 us (4%)
    pallas_call x1, Pallas kernels, fused(): pl.pallas_call(partial(fused_kernel, groups, parts), in_specs=[pl.BlockSp...  95.8 us
    unnamed x9, local copies, waits for them, and re-layouts  4.32 us

profile of v4, /device:TPU:0, one launch (start us, length us, event | category | flops | bytes accessed | tf_op | source)
XLA Modules:
  0.0 100.8 jit_solution(2415390330674878864)
XLA Ops:
  0.6 0.0 copy-start
  0.6 1.0 %copy-done = bf16[1,2048,128]{2,1,0:T(8,128)(2,1)S(1)} copy-done((bf16[1,2048,128]{2,1,0:T(8,128)(2,1)S(1)}, bf16[1,2048,128]{2,1,0:T(8,128)(2,1)}, u32[]{:S(2)}) %copy-start) | copy-done | bytes 524312
  1.7 0.0 copy-start.1
  1.7 0.7 copy-done.1
  2.4 95.8 %shard_map.94 = (f32[8,256,128]{2,1,0:T(8,128)}, bf16[8,256,128]{2,1,0:T(8,128)(2,1)S(1)}, bf16[8,256,128]{2,1,0:T(8,128)(2,1)S(1)}) custom-call(f32[36,8]{1,0:T(8,128)S(1)} %copy-done.1, bf16[9,256,256]{2,1,0:T(8,128)(2,1)} %constant.7.clone.high_ref, bf16[9,256,256]{2,1,0:T(8,128)(2,1)} %constant.8.clone.low_ref, f32[8,256,128]{2,1,0:T(8,128)} %bitcast.11, ...), custom_call_target="tpu_custom_call" | custom-call | tf_op jit(solution)/shard_map/pallas_call | solution.py:306
  98.2 0.0 copy-start.2
  98.2 0.8 copy.13
  99.0 0.8 copy.14
  99.8 0.0 copy-done.2
  99.8 1.0 copy.15
Async XLA Ops:
  0.6 1.0 %copy-start = (bf16[1,2048,128]{2,1,0:T(8,128)(2,1)S(1)}, bf16[1,2048,128]{2,1,0:T(8,128)(2,1)}, u32[]{:S(2)}) copy-start(bf16[1,2048,128]{2,1,0:T(8,128)(2,1)} %param.7) | copy-start | bytes 1572868
  1.7 0.7 copy-start.1
  98.2 1.6 %copy-start.2 = (f32[8,256,128]{2,1,0:T(8,128)S(1)}, f32[8,256,128]{2,1,0:T(8,128)}, u32[]{:S(2)}) copy-start(f32[8,256,128]{2,1,0:T(8,128)} %get-tuple-element.8) | copy-start | bytes 3145732
